TPU v7x, 32 devices: a whole 2x2x4 slice. The times are simulated.
32 devices in a mesh: lat: 8 (over z, x), ch: 4 (over y, core).
Axes of the slice: x: 2, y: 2, z: 4, core: 2. Of those that a mesh axis runs over, the one named last changes fastest.
Arguments:
- tokens: bfloat16 [1, 16, 8, 69120], P(None, 'lat', 'ch'), may hold values from -6 to 6
- cotangent: bfloat16 [1, 16, 8, 69120], P(None, 'lat', 'ch'), may hold values from -6 to 6
- first_weight: bfloat16 [2, 8, 96, 96], P(None, 'ch'), may hold values from -0.4375 to 0.4375
- first_bias: bfloat16 [2, 8, 96], P(None, 'ch'), may hold values from -6 to 6
- second_weight: bfloat16 [2, 8, 96, 96], P(None, 'ch'), may hold values from -0.4375 to 0.4375
- relu_mask: int32 [1, 2, 8, 256, 1536], P(None, None, 'ch', 'lat'), may hold values 0 or 1
- shrink_mask: int32 [1, 2, 8, 256, 1536], P(None, None, 'ch', 'lat'), may hold values 0 or 1
Outputs:
- token_gradient: bfloat16 [1, 16, 8, 69120], P(None, 'lat', 'ch')
- first_gradient: float32 [2, 8, 96, 96], P(None, 'ch')
- bias_gradient: float32 [2, 8, 96], P(None, 'ch')
- second_gradient: float32 [2, 8, 96, 96], P(None, 'ch')
All inputs are finite; a program needn't handle non-finite values. No bound on the sum of `relu_mask` or of `shrink_mask` on one device may be relied on, other than what follows from the above.
Results may differ from a plain program's by a relative error of at most 0.0093.
Values may be sent and summed in bfloat16 or wider, within the bound.
No kernel may reach another device: no remote copies, remote signals or barrier semaphores. Data moves between devices by JAX's collectives and lax.ppermute only.
A program may use at most 64 MiB of HBM per device.

v0:
```python
import functools
import math

import jax
import jax.numpy as jnp
import numpy as np
from jax import lax
from jax.experimental import pallas as pl
from jax.experimental.pallas import tpu as pltpu
from jax.sharding import PartitionSpec as P


WAVES = 256
PAIRWISE = (2, 4, 8)
GO_ORDER = (0, 7, 5, 6, 3, 4, 2, 1)
BACK_ORDER = (0, 5, 7, 3, 4, 6, 2, 1)
BF16 = jnp.bfloat16
F32 = jnp.float32


def group_of(wave_dev):
    return 8 if wave_dev % 8 == 0 else wave_dev


def east_rows(count, waves, owners):
    wave_dev = waves // owners
    group = group_of(wave_dev)
    phase = np.outer(np.arange(waves), np.arange(count)) % count * (2.0 * math.pi / count)
    table = np.stack([np.cos(phase), -np.sin(phase)]) / math.sqrt(count)
    table = table.reshape(2, owners, wave_dev // group, group, count)
    return table.transpose(1, 2, 0, 3, 4).reshape(2 * waves, count)


def north_rows(owners, rows, group):
    cells = owners * rows
    phase = np.outer(np.arange(cells), np.arange(cells)) % cells * (2.0 * math.pi / cells)
    cosine, sine = np.cos(phase) / math.sqrt(cells), np.sin(phase) / math.sqrt(cells)
    table = np.stack([np.stack([cosine, sine], 1), np.stack([-sine, cosine], 1)])
    table = table.reshape(2, cells, 2, owners, rows)
    full = np.einsum("tqsjr,kl->tqkrjsl", table, np.eye(group))
    return full.reshape(2 * group * cells, rows * owners * 2 * group)


def distances(order, owners):
    return [d for d in order if d < owners]


def first_distance(owners):
    return distances(GO_ORDER, owners)[1]


def dot(left, right, form=((1,), (0,))):
    return lax.dot_general(left, right, (form, ((), ())), preferred_element_type=F32)


ROWS, COLS = ((0,), (0,)), ((1,), (1,))


def mix_core(spec_ref, table_ref, back_ref, weight_ref, bias_ref, relu_ref, shrink_ref,
             lay_ref, result_ref):
    groups = spec_ref.shape[1]
    blocks, block = lay_ref.shape[1], lay_ref.shape[3] // 2
    half = table_ref.shape[0] // 2

    def side(value, n):
        return value[:, n * block : (n + 1) * block]

    for f in range(2):
        for g in range(groups):
            modes = dot(table_ref[...], spec_ref[f, g]).astype(BF16)
            for n in range(blocks):
                lay_ref[f, n, g * half : (g + 1) * half, :] = jnp.concatenate(
                    [side(modes[:half], n), side(modes[half:], n)], axis=1)
    products, biases = ([], []), []
    for n in range(blocks):
        modes, up = lay_ref[0, n], lay_ref[1, n] * shrink_ref[n]
        keep = relu_ref[n].astype(F32)
        one, two = weight_ref[0, n], weight_ref[1, n]
        hidden = (keep * (dot(modes, one) + bias_ref[n : n + 1, :].astype(F32))).astype(BF16)
        inner = (keep * dot(up, two, COLS)).astype(BF16)
        lay_ref[0, n] = dot(inner, one, COLS).astype(BF16)
        products[0].append(dot(modes, inner, ROWS))
        products[1].append(dot(hidden, up, ROWS))
        biases.append(jnp.sum(inner.astype(F32), axis=0, keepdims=True))
    for g in range(groups):
        at = slice(g * half, (g + 1) * half)
        parts = [jnp.concatenate([side(lay_ref[0, n, at, :], s) for n in range(blocks)], axis=1)
                 for s in range(2)]
        result_ref[g] = dot(back_ref[...], jnp.concatenate(parts, axis=0)).astype(BF16)

    def split(product):
        real = side(product[:block], 0) + side(product[block:], 1)
        return real, side(product[:block], 1) - side(product[block:], 0)

    rows = []
    for some in products:
        pairs = [split(product) for product in some]
        rows.append(jnp.concatenate([pair[s] for s in range(2) for pair in pairs], axis=1))
    bias = jnp.concatenate([side(row, s) for s in range(2) for row in biases], axis=1)
    return jnp.concatenate(rows, axis=0), bias


def mix_whole_kernel(*refs):
    spec_ref, result_ref, grad_ref, bias_ref, lay_ref = refs[0], *refs[7:]
    gathered, bias = mix_core(spec_ref, *refs[1:7], lay_ref, result_ref)
    grad_ref[...] = gathered.astype(BF16)
    bias_ref[...] = bias.astype(BF16)


def ready_kernel(geo, relu_in, shrink_in, first_in, second_in, bias_in,
                 relu_out, shrink_out, weight_out, bias_out):
    groups, group, north, blocks, block = geo
    for source, out in ((relu_in, relu_out), (shrink_in, shrink_out)):
        for n in range(blocks):
            planes = [source[0, s, n].astype(F32).astype(BF16) for s in range(2)]
            for q in range(north):
                at = slice(q * block, (q + 1) * block)
                row = jnp.concatenate([plane[:, at] for plane in planes], axis=1)
                for g in range(groups):
                    start = (g * north + q) * group
                    out[n, start : start + group, :] = row[g * group : (g + 1) * group]
    for index, source in enumerate((first_in, second_in)):
        for n in range(blocks):
            real, imag = source[0, n], source[1, n]
            weight_out[index, n, :block, :] = jnp.concatenate([real, imag], axis=1)
            weight_out[index, n, block:, :] = jnp.concatenate([-imag, real], axis=1)
    for n in range(blocks):
        parts = [bias_in[s, n : n + 1, :] for s in range(2)]
        bias_out[n : n + 1, :] = jnp.concatenate(parts, axis=1)


def send_kernel(geo, tokens_ref, cotangent_ref, east_ref, out_ref, grid_ref,
                flat_ref, fields_ref, table_ref, sems):
    owners, block, units, padded, tiles, unit = geo
    rows, blocks = tokens_ref.shape[:2]
    field = rows * blocks * block
    span = out_ref.shape[0]
    copies = []
    for f, source in enumerate((tokens_ref, cotangent_ref)):
        for h in range(rows):
            copies.append((source.at[h], fields_ref.at[f, h]))
    if span < east_ref.shape[0]:
        start = pl.multiple_of((lax.axis_index("lat") ^ first_distance(owners)) * span, span)
        copies.append((east_ref.at[pl.ds(start, span)], table_ref))
    else:
        copies.append((east_ref, table_ref))
    copies = [pltpu.make_async_copy(a, b, sems.at[i]) for i, (a, b) in enumerate(copies)]
    for copy in copies:
        copy.start()
    for f in range(2):
        places = []
        for h in range(rows):
            copies[f * rows + h].wait()
            flat = fields_ref[f, h].astype(F32)
            flat_ref[f, h] = flat.reshape(blocks, units * tiles, 128)
            for n in range(blocks):
                parts = [flat_ref[f, h, n, pl.ds(c, units, stride=tiles), :].astype(BF16)
                         for c in range(tiles)]
                places.append(jnp.concatenate(parts, axis=1))
        for r in range(unit):
            piece = [place[:, r * block : (r + 1) * block] for place in places]
            at = slice(f * field, (f + 1) * field)
            grid_ref[r * padded : r * padded + units, at] = jnp.concatenate(piece, axis=1)
            if padded > units:
                grid_ref[r * padded + units : (r + 1) * padded, at] = jnp.zeros(
                    (padded - units, field), BF16)
    copies[-1].wait()
    out_ref[...] = dot(table_ref[...], grid_ref[...]).astype(BF16)


def rest_kernel(owners, east_ref, grid_ref, *refs):
    outs, table_ref, sems = refs[:-2], refs[-2], refs[-1]
    span = outs[0].shape[0]
    me = lax.axis_index("lat")
    copies = []
    for d, distance in enumerate(d for d in distances(GO_ORDER, owners) if d != first_distance(owners)):
        start = pl.multiple_of((me ^ distance) * span, span)
        copies.append(pltpu.make_async_copy(
            east_ref.at[pl.ds(start, span)], table_ref.at[pl.ds(d * span, span)], sems.at[d]))
    for copy in copies:
        copy.start()
    for copy in copies:
        copy.wait()
    waves = dot(table_ref[...], grid_ref[...]).astype(BF16)
    for d, out in enumerate(outs):
        out[...] = waves[d * span : (d + 1) * span]


def mix_kernel(geo, *refs):
    owners, groups, rows, width, per = geo
    pieces, consts, outs = refs[:owners], refs[owners : owners + 6], refs[owners + 6 : -4]
    spec_ref, lay_ref, back_ref, grad_ref = refs[-4:]
    me = lax.axis_index("lat")
    part = pieces[0].shape[0] // groups
    for d, distance in enumerate(distances(GO_ORDER, owners)):
        for f in range(2):
            for r in range(rows):
                lane = (f * rows + r) * width
                value = pieces[d][:, lane : lane + width]
                start = pl.multiple_of((r * owners + (me ^ distance)) * part, part)
                for g in range(groups):
                    spec_ref[f, g, pl.ds(start, part), :] = value[g * part : (g + 1) * part]
    grad_ref[...], bias = mix_core(spec_ref, *consts, lay_ref, back_ref)
    span, lanes = part * groups, outs[0].shape[1]
    tiles = rows * width // lanes
    body = tiles * span
    rest = outs[0].shape[0] - body - tiles * per - tiles
    biases = [bias[:, t * lanes : (t + 1) * lanes] for t in range(tiles)]
    biases.append(jnp.zeros((rest, lanes), F32))
    for d, distance in enumerate(distances(BACK_ORDER, owners)):
        for g in range(groups):
            parts = []
            for r in range(rows):
                start = pl.multiple_of((r * owners + (me ^ distance)) * part, part)
                parts.append(back_ref[g, pl.ds(start, part), :])
            row = jnp.concatenate(parts, axis=1)
            for t in range(tiles):
                start = t * span + g * part
                outs[d][start : start + part, :] = row[:, t * lanes : (t + 1) * lanes]
        start = pl.multiple_of((me ^ distance) * per, per)
        chunk = grad_ref[pl.ds(start, per), :]
        parts = [chunk[:, t * lanes : (t + 1) * lanes] for t in range(tiles)]
        outs[d][body:, :] = jnp.concatenate(parts + biases, axis=0).astype(BF16)


def sum_kernel(geo, *refs):
    body, per, tiles, block, factor = geo
    pieces, out, bias_ref = refs[:-2], refs[-2], refs[-1]
    total = pieces[0][body:, :].astype(F32)
    for piece in pieces[1:]:
        total = total + piece[body:, :].astype(F32)
    total = total * factor
    chunk = total[: tiles * per].astype(BF16)
    for d in range(out.shape[0]):
        out[d] = chunk
    blocks = bias_ref.shape[1]
    lead = [total[tiles * per + t : tiles * per + t + 1, :] for t in range(tiles)]
    lead = jnp.concatenate(lead, axis=1)
    for p in range(2):
        for n in range(blocks):
            at = slice((p * blocks + n) * block, (p * blocks + n + 1) * block)
            bias_ref[p, n : n + 1, :] = lead[:, at]


def token_kernel(geo, east_ref, grid_ref, *refs):
    owners, block, units, padded, tiles, unit = geo
    pieces, out, (wave_ref, flat_ref) = refs[:-3], refs[-3], refs[-2:]
    if len(pieces) == 1:
        wave_ref[...] = pieces[0][...]
    else:
        me = lax.axis_index("lat")
        span = wave_ref.shape[0] // owners
        for d, distance in enumerate(distances(BACK_ORDER, owners)):
            start = pl.multiple_of((me ^ distance) * span, span)
            for t in range(wave_ref.shape[1] // 128):
                at = slice(t * 128, (t + 1) * 128)
                wave_ref[pl.ds(start, span), at] = pieces[d][t * span : (t + 1) * span, :]
    field = wave_ref.shape[1]
    token = dot(east_ref[...], wave_ref[...]) + grid_ref[:, field:].astype(F32)
    rows, blocks = out.shape[:2]
    for h in range(rows):
        for n in range(blocks):
            p = h * blocks + n
            parts = [token[r * padded : r * padded + units, p * block : (p + 1) * block]
                     for r in range(unit)]
            place = jnp.concatenate(parts, axis=1)
            for c in range(tiles):
                flat_ref[h, n, pl.ds(c, units, stride=tiles), :] = place[:, c * 128 : (c + 1) * 128]
        out[h] = flat_ref[h].reshape(blocks, units * tiles * 128).astype(BF16)


def final_kernel(block, total_ref, first_ref, second_ref):
    blocks = first_ref.shape[1]
    tiles = 2 * blocks * block // total_ref.shape[2]
    owners, per = total_ref.shape[0], total_ref.shape[1] // tiles
    for j in range(owners):
        chunk = total_ref[j].astype(F32)
        chunk = jnp.concatenate([chunk[t * per : (t + 1) * per] for t in range(tiles)], axis=1)
        out = first_ref if j * per < block else second_ref
        start = j * per % block
        for p in range(2):
            for n in range(blocks):
                at = slice((p * blocks + n) * block, (p * blocks + n + 1) * block)
                out[p, n, start : start + per, :] = chunk[:, at]


VMEM = pl.BlockSpec(memory_space=pltpu.VMEM)


def call(kernel, args, shapes, scratch=(), in_hbm=0):
    shapes = [shape if isinstance(shape[0], tuple) else (shape, BF16) for shape in shapes]
    kept = [pltpu.with_memory_space_constraint(arg, pltpu.HBM) for arg in args[:in_hbm]]
    return pl.pallas_call(
        kernel,
        out_shape=[jax.ShapeDtypeStruct(shape, kind) for shape, kind in shapes],
        in_specs=[pl.BlockSpec(memory_space=pltpu.HBM)] * in_hbm + [VMEM] * (len(args) - in_hbm),
        out_specs=[VMEM] * len(shapes),
        scratch_shapes=list(scratch),
        compiler_params=pltpu.CompilerParams(vmem_limit_bytes=24 << 20),
    )(*kept, *args[in_hbm:])


def swap(order, pieces, owners):
    got = []
    for d, piece in zip(distances(order, owners), pieces):
        pairs = [(i, i ^ d) for i in range(owners)]
        got.append(lax.ppermute(piece, "lat", pairs) if d else piece)
    return got


def local(tokens, cotangent, first_weight, first_bias, second_weight, relu_mask, shrink_mask):
    batches, rows, blocks, flat_east = tokens.shape
    block = first_weight.shape[2]
    cells = flat_east // block
    owners = lax.axis_size("lat")
    wave_dev = WAVES // owners
    group = group_of(wave_dev)
    groups = wave_dev // group
    north = rows * owners
    width = blocks * block
    field = rows * width
    span = 2 * wave_dev
    factor = 1.0 / math.sqrt(north * WAVES)

    lanes = math.lcm(block, 128)
    unit, tiles = lanes // block, lanes // 128
    units = cells // unit
    padded = -(-units // 16) * 16
    geo = (owners, block, units, padded, tiles, unit)
    east = east_rows(cells, WAVES, owners).reshape(2 * WAVES, units, unit).swapaxes(1, 2)
    east = np.pad(east, ((0, 0), (0, 0), (0, padded - units))).reshape(2 * WAVES, unit * padded)
    east_back = jnp.asarray(east.T, BF16)
    east = jnp.asarray(east, BF16)
    table = north_rows(owners, rows, group)
    forward = jnp.asarray(table, BF16)
    backward = jnp.asarray(table.T, BF16)

    def by_mode(mask):
        mask = mask.astype(BF16).reshape(2, blocks, groups, group, north, block)
        return mask.transpose(1, 2, 4, 3, 0, 5).reshape(blocks, wave_dev * north, 2 * block)

    def as_real(weight):
        real, imag = weight[0], weight[1]
        top = jnp.concatenate([real, imag], axis=2)
        return jnp.concatenate([top, jnp.concatenate([-imag, real], axis=2)], axis=1)

    per = -(-2 * block // owners)
    pairwise = (
        owners in PAIRWISE and group % 8 == 0 and per * owners == 2 * block and field % 128 == 0
    )

    flat = (rows, blocks, flat_east)
    modes = (blocks, wave_dev * north, 2 * block)
    spectra = (groups, rows * owners * 2 * group, width)
    lay = pltpu.VMEM((2,) + modes, BF16)
    ahead = span if pairwise else owners * span
    waves, grid = call(
        functools.partial(send_kernel, geo),
        [tokens.reshape(flat), cotangent.reshape(flat), east],
        [(ahead, 2 * field), (unit * padded, 2 * field)],
        [pltpu.VMEM((2, rows, blocks, units * tiles, 128), F32), pltpu.VMEM((2,) + flat, BF16),
         pltpu.VMEM((ahead, unit * padded), BF16), pltpu.SemaphoreType.DMA((2 * rows + 1,))],
        3,
    )

    if pairwise:
        own, *rest = call(
            functools.partial(rest_kernel, owners), [east, grid],
            [(span, 2 * field)] * (owners - 1),
            [pltpu.VMEM(((owners - 1) * span, unit * padded), BF16),
             pltpu.SemaphoreType.DMA((owners - 1,))], 1,
        )
        waves = [own, waves] + rest
        ready = call(
            functools.partial(ready_kernel, (groups, group, north, blocks, block)),
            [relu_mask, shrink_mask, first_weight, second_weight, first_bias],
            [modes, modes, (2, blocks, 2 * block, 2 * block), (blocks, 2 * block)],
        )
        sides = field // 128
        body = sides * span
        extra = -(-sides * (per + 1) // 16) * 16
        relu, shrink, weights, bias = ready
        pieces = call(
            functools.partial(mix_kernel, (owners, groups, rows, width, per)),
            swap(GO_ORDER, waves, owners) + [forward, backward, weights, bias, relu, shrink],
            [(body + extra, 128)] * owners,
            [pltpu.VMEM((2,) + spectra, BF16), lay, pltpu.VMEM(spectra, BF16),
             pltpu.VMEM((2 * block, field), F32)],
        )
        pieces = swap(BACK_ORDER, pieces, owners)
        chunk, bias_grad = call(
            functools.partial(sum_kernel, (body, per, sides, block, factor)), pieces,
            [(owners, sides * per, 128), ((2, blocks, block), F32)],
        )
        totals = lax.all_to_all(chunk, "lat", split_axis=0, concat_axis=0, tiled=True)
    else:
        weights = jnp.stack([as_real(first_weight), as_real(second_weight)])
        bias = first_bias.swapaxes(0, 1).reshape(blocks, 2 * block)
        waves = waves.reshape(owners, span, 2 * field)
        waves = lax.all_to_all(waves, "lat", split_axis=0, concat_axis=0, tiled=True)
        waves = waves.reshape(owners, groups, 2 * group, 2, rows, width)
        waves = waves.transpose(3, 1, 4, 0, 2, 5).reshape((2,) + spectra)
        sent, grads, biases = call(
            mix_whole_kernel,
            [waves, forward, backward, weights, bias, by_mode(relu_mask), by_mode(shrink_mask)],
            [spectra, (2 * block, field), (1, field)], [lay],
        )
        sent = sent.reshape(groups, rows, owners, 2 * group, width).transpose(2, 0, 3, 1, 4)
        sent = sent.reshape(owners, span, field)
        grads = jnp.pad(grads, ((0, owners * per - 2 * block), (0, 0)))
        biases = jnp.broadcast_to(biases[None], (owners, 1, field))
        sent = jnp.concatenate([sent, grads.reshape(owners, per, field), biases], axis=1)
        returned = lax.all_to_all(sent, "lat", split_axis=0, concat_axis=0, tiled=True)
        pieces = [returned[:, :span].reshape(owners * span, field)]
        chunk = jnp.sum(returned[:, span:].astype(F32), axis=0) * factor
        chunk = jnp.broadcast_to(chunk.astype(BF16)[None], (owners,) + chunk.shape)
        totals = lax.all_to_all(chunk, "lat", split_axis=0, concat_axis=0, tiled=True)

    (token,) = call(
        functools.partial(token_kernel, geo), [east_back, grid] + pieces, [flat],
        [pltpu.VMEM((owners * span, field), BF16),
         pltpu.VMEM(flat[:2] + (units * tiles, 128), F32)],
    )
    token = token.reshape(batches, rows, blocks, flat_east)
    if pairwise:
        matrix = ((2, blocks, block, block), F32)
        first, second = call(functools.partial(final_kernel, block), [totals], [matrix, matrix])
        return (token, first, bias_grad, second)
    totals = totals.astype(F32)
    grads = totals[:, :per].reshape(owners * per, field)[: 2 * block]
    grads = grads.reshape(2, block, 2, blocks, block).transpose(0, 2, 3, 1, 4)
    bias_grad = totals[0, per].reshape(2, blocks, block)
    return (token, grads[0], bias_grad, grads[1])


def solution(mesh):
    step = mapped(local, mesh)
    return step


def mapped(body, mesh):
    return jax.shard_map(
        body,
        mesh=mesh,
        in_specs=(
            P(None, "lat", "ch", None),
            P(None, "lat", "ch", None),
            P(None, "ch", None, None),
            P(None, "ch", None),
            P(None, "ch", None, None),
            P(None, None, "ch", "lat", None),
            P(None, None, "ch", "lat", None),
        ),
        out_specs=(
            P(None, "lat", "ch", None),
            P(None, "ch", None, None),
            P(None, "ch", None),
            P(None, "ch", None, None),
        ),
        check_vma=False,
    )
```

profile of v0, /device:TPU:0, one launch (start us, length us, event | category | flops | bytes accessed | tf_op | source)
XLA Modules:
  0.0 57.8 jit_solution(10681238806643899351)
XLA Ops:
  0.6 3.0 %shard_map.138 = (bf16[64,768]{1,0:T(8,128)(2,1)S(1)}, bf16[768,768]{1,0:T(8,128)(2,1)S(1)}) custom-call(bf16[2,2,69120]{2,1,0:T(2,128)(2,1)} %bitcast.3, bf16[2,2,69120]{2,1,0:T(2,128)(2,1)} %bitcast.4, bf16[512,768]{1,0:T(8,128)(2,1)} %constant.9.clone.east_ref), custom_call_target="tpu_custom_call" | custom-call | tf_op jit(solution)/shard_map/pallas_call | solution.py:293
  3.7 6.1 %collective-permute-start = (bf16[64,768]{1,0:T(8,128)(2,1)S(1)}, bf16[64,768]{1,0:T(8,128)(2,1)S(1)}, u32[]{:S(2)}, u32[]{:S(2)}) collective-permute-start(bf16[64,768]{1,0:T(8,128)(2,1)S(1)} %get-tuple-element.31), channel_id=1, source_target_pairs={{0,28},{4,24},{8,20},{12,16},{16,12},{20,8},{24,4},{28,0},{1,29},{... | collective-permute-start | bytes 294920 | tf_op jit(solution)/shard_map/ppermute | solution.py:307
  9.8 1.9 %shard_map.139 = (bf16[64,768]{1,0:T(8,128)(2,1)S(1)}, bf16[64,768]{1,0:T(8,128)(2,1)S(1)}, bf16[64,768]{1,0:T(8,128)(2,1)S(1)}, bf16[64,768]{1,0:T(8,128)(2,1)S...) custom-call(bf16[512,768]{1,0:T(8,128)(2,1)} %constant.9.clone.east_ref, ...), custom_call_target="tpu_custom_call" | custom-call | tf_op jit(solution)/shard_map/pallas_call | solution.py:293
  11.8 1.9 %collective-permute-start.2 = (bf16[64,768]{1,0:T(8,128)(2,1)S(1)}, bf16[64,768]{1,0:T(8,128)(2,1)S(1)}, u32[]{:S(2)}, u32[]{:S(2)}) collective-permute-start(bf16[64,768]{1,0:T(8,128)(2,1)S(1)} %get-tuple-element.33), channel_id=1, source_target_pairs={{0,24},{4,28},{8,16},{12,20},{16,8},{20,12},{24,0},{28,4},{1,25},{... | collective-permute-start | bytes 294920 | tf_op jit(solution)/shard_map/ppermute | solution.py:307
  13.7 2.5 %collective-permute-start.3 = (bf16[64,768]{1,0:T(8,128)(2,1)S(1)}, bf16[64,768]{1,0:T(8,128)(2,1)S(1)}, u32[]{:S(2)}, u32[]{:S(2)}) collective-permute-start(bf16[64,768]{1,0:T(8,128)(2,1)S(1)} %get-tuple-element.34), channel_id=1, source_target_pairs={{0,12},{4,8},{8,4},{12,0},{16,28},{20,24},{24,20},{28,16},{1,13},{... | collective-permute-start | bytes 294920 | tf_op jit(solution)/shard_map/ppermute | solution.py:307
  16.2 0.3 collective-permute-start.4
  16.6 1.1 %collective-permute-start.5 = (bf16[64,768]{1,0:T(8,128)(2,1)S(1)}, bf16[64,768]{1,0:T(8,128)(2,1)S(1)}, u32[]{:S(2)}, u32[]{:S(2)}) collective-permute-start(bf16[64,768]{1,0:T(8,128)(2,1)S(1)} %get-tuple-element.36), channel_id=1, source_target_pairs={{0,8},{4,12},{8,0},{12,4},{16,24},{20,28},{24,16},{28,20},{1,9},{5... | collective-permute-start | bytes 294920 | tf_op jit(solution)/shard_map/ppermute | solution.py:307
  17.7 4.5 %collective-permute-done.1.refs_2_ = bf16[64,768]{1,0:T(8,128)(2,1)S(1)} collective-permute-done((bf16[64,768]{1,0:T(8,128)(2,1)S(1)}, bf16[64,768]{1,0:T(8,128)(2,1)S(1)}, u32[]{:S(2)}, u32[]{:S(2)}) %collective-permute-start.1) | collective-permute-done | bytes 98336 | tf_op jit(solution)/shard_map/ppermute | solution.py:307
  22.2 1.0 %collective-permute-start.6 = (bf16[64,768]{1,0:T(8,128)(2,1)S(1)}, bf16[64,768]{1,0:T(8,128)(2,1)S(1)}, u32[]{:S(2)}, u32[]{:S(2)}) collective-permute-start(bf16[64,768]{1,0:T(8,128)(2,1)S(1)} %get-tuple-element.37), channel_id=1, source_target_pairs={{0,4},{4,0},{8,12},{12,8},{16,20},{20,16},{24,28},{28,24},{1,5},{5... | collective-permute-start | bytes 294920 | tf_op jit(solution)/shard_map/ppermute | solution.py:307
  23.2 0.4 shard_map.140
  23.7 2.8 %collective-permute-done.4.refs_5_ = bf16[64,768]{1,0:T(8,128)(2,1)S(1)} collective-permute-done((bf16[64,768]{1,0:T(8,128)(2,1)S(1)}, bf16[64,768]{1,0:T(8,128)(2,1)S(1)}, u32[]{:S(2)}, u32[]{:S(2)}) %collective-permute-start.4) | collective-permute-done | bytes 98336 | tf_op jit(solution)/shard_map/ppermute | solution.py:307
  26.9 2.2 %shard_map.141 = (bf16[272,128]{1,0:T(8,128)(2,1)S(1)}, bf16[272,128]{1,0:T(8,128)(2,1)S(1)}, bf16[272,128]{1,0:T(8,128)(2,1)S(1)}, bf16[272,128]{1,0:T(8,128)(2...) custom-call(bf16[64,768]{1,0:T(8,128)(2,1)S(1)} %get-tuple-element.3, ...), custom_call_target="tpu_custom_call" | custom-call | tf_op jit(solution)/shard_map/pallas_call | solution.py:293
  29.2 2.8 %collective-permute-start.8 = (bf16[272,128]{1,0:T(8,128)(2,1)S(1)}, bf16[272,128]{1,0:T(8,128)(2,1)S(1)}, u32[]{:S(2)}, u32[]{:S(2)}) collective-permute-start(bf16[272,128]{1,0:T(8,128)(2,1)S(1)} %get-tuple-element.44), channel_id=1, source_target_pairs={{0,28},{4,24},{8,20},{12,16},{16,12},{20,8},{24,4},{28,0},{1,29},{... | collective-permute-start | bytes 208904 | tf_op jit(solution)/shard_map/ppermute | solution.py:307
  32.0 2.0 %collective-permute-start.9 = (bf16[272,128]{1,0:T(8,128)(2,1)S(1)}, bf16[272,128]{1,0:T(8,128)(2,1)S(1)}, u32[]{:S(2)}, u32[]{:S(2)}) collective-permute-start(bf16[272,128]{1,0:T(8,128)(2,1)S(1)} %get-tuple-element.45), channel_id=1, source_target_pairs={{0,12},{4,8},{8,4},{12,0},{16,28},{20,24},{24,20},{28,16},{1,13},{... | collective-permute-start | bytes 208904 | tf_op jit(solution)/shard_map/ppermute | solution.py:307
  34.1 0.4 collective-permute-start.10
  34.5 2.2 %collective-permute-start.11 = (bf16[272,128]{1,0:T(8,128)(2,1)S(1)}, bf16[272,128]{1,0:T(8,128)(2,1)S(1)}, u32[]{:S(2)}, u32[]{:S(2)}) collective-permute-start(bf16[272,128]{1,0:T(8,128)(2,1)S(1)} %get-tuple-element.47), channel_id=1, source_target_pairs={{0,24},{4,28},{8,16},{12,20},{16,8},{20,12},{24,0},{28,4},{1,25},{... | collective-permute-start | bytes 208904 | tf_op jit(solution)/shard_map/ppermute | solution.py:307
  36.7 0.7 %collective-permute-done.7.refs_1_ = bf16[272,128]{1,0:T(8,128)(2,1)S(1)} collective-permute-done((bf16[272,128]{1,0:T(8,128)(2,1)S(1)}, bf16[272,128]{1,0:T(8,128)(2,1)S(1)}, u32[]{:S(2)}, u32[]{:S(2)}) %collective-permute-start.7) | collective-permute-done | bytes 69664 | tf_op jit(solution)/shard_map/ppermute | solution.py:307
  37.5 2.0 %collective-permute-start.13 = (bf16[272,128]{1,0:T(8,128)(2,1)S(1)}, bf16[272,128]{1,0:T(8,128)(2,1)S(1)}, u32[]{:S(2)}, u32[]{:S(2)}) collective-permute-start(bf16[272,128]{1,0:T(8,128)(2,1)S(1)} %get-tuple-element.49), channel_id=1, source_target_pairs={{0,4},{4,0},{8,12},{12,8},{16,20},{20,16},{24,28},{28,24},{1,5},{5... | collective-permute-start | bytes 208904 | tf_op jit(solution)/shard_map/ppermute | solution.py:307
  39.5 3.5 %collective-permute-done.10.refs_4_ = bf16[272,128]{1,0:T(8,128)(2,1)S(1)} collective-permute-done((bf16[272,128]{1,0:T(8,128)(2,1)S(1)}, bf16[272,128]{1,0:T(8,128)(2,1)S(1)}, u32[]{:S(2)}, u32[]{:S(2)}) %collective-permute-start.10) | collective-permute-done | bytes 69664 | tf_op jit(solution)/shard_map/ppermute | solution.py:307
  43.3 0.7 %shard_map.143 = (bf16[8,72,128]{2,1,0:T(8,128)(2,1)}, f32[2,2,96]{2,1,0:T(2,128)}) custom-call(bf16[272,128]{1,0:T(8,128)(2,1)S(1)} %get-tuple-element.42.refs_0_, bf16[272,128]{1,0:T(8,128)(2,1)S(1)} %collective-permute-done.7.refs_1_, bf16[272,128]{1,0:T(8,128)(2,1)S(1)} %collective-permute-done.8.refs_2_, ...), custom_call_target="tpu_custom_call" | custom-call | tf_op jit(solution)/shard_map/pallas_call | solution.py:293
  44.0 5.5 %all-to-all-start = ((bf16[8,72,128]{2,1,0:T(8,128)(2,1)}), bf16[8,72,128]{2,1,0:T(8,128)(2,1)S(1)}, u32[]{:S(2)}, u32[]{:S(2)}) async-start(bf16[8,72,128]{2,1,0:T(8,128)(2,1)} %get-tuple-element.50), calls=%async_computation | async-start | bytes 294912 | tf_op jit(solution)/shard_map/all_to_all | solution.py:395
  49.5 2.2 %shard_map.142 = bf16[2,2,69120]{2,1,0:T(2,128)(2,1)} custom-call(bf16[768,512]{1,0:T(8,128)(2,1)S(1)} %copy-done.2, bf16[768,768]{1,0:T(8,128)(2,1)S(1)} %get-tuple-element.29.grid_ref, bf16[272,128]{1,0:T(8,128)(2,1)S(1)} %get-tuple-element.42.refs_0_, bf16[272,128]{1,0:T(8,128)(2,1)S(1)} %collective-permute-done.7.refs_1_, ...), custom_call_target="tpu_custom_call" | custom-call | tf_op jit(solution)/shard_map/pallas_call | solution.py:293
  51.7 5.2 %all-to-all-done.total_ref = bf16[8,72,128]{2,1,0:T(8,128)(2,1)S(1)} async-done(((bf16[8,72,128]{2,1,0:T(8,128)(2,1)}), bf16[8,72,128]{2,1,0:T(8,128)(2,1)S(1)}, u32[]{:S(2)}, u32[]{:S(2)}) %all-to-all-start) | async-done | bytes 147488 | tf_op jit(solution)/shard_map/all_to_all | solution.py:395
  56.9 0.8 %shard_map.144 = (f32[2,2,96,96]{3,2,1,0:T(8,128)}, f32[2,2,96,96]{3,2,1,0:T(8,128)}) custom-call(bf16[8,72,128]{2,1,0:T(8,128)(2,1)S(1)} %all-to-all-done.total_ref), custom_call_target="tpu_custom_call" | custom-call | tf_op jit(solution)/shard_map/pallas_call | solution.py:293
  (29 shorter events, 1.0 us)
Async XLA Ops:
  3.7 19.6 %copy-start = (s32[1,2,2,32,1536]{4,3,2,1,0:T(8,128)S(1)}, s32[1,2,2,32,1536]{4,3,2,1,0:T(8,128)}, u32[]{:S(2)}) copy-start(s32[1,2,2,32,1536]{4,3,2,1,0:T(8,128)} %relu_in.1) | copy-start | bytes 2359300
  3.7 19.5 %copy-start.1 = (s32[1,2,2,32,1536]{4,3,2,1,0:T(8,128)S(1)}, s32[1,2,2,32,1536]{4,3,2,1,0:T(8,128)}, u32[]{:S(2)}) copy-start(s32[1,2,2,32,1536]{4,3,2,1,0:T(8,128)} %shrink_in.1) | copy-start | bytes 2359300
  3.7 19.5 %copy-start.5 = (bf16[2,2,96,96]{3,2,1,0:T(8,128)(2,1)S(1)}, bf16[2,2,96,96]{3,2,1,0:T(8,128)(2,1)}, u32[]{:S(2)}) copy-start(bf16[2,2,96,96]{3,2,1,0:T(8,128)(2,1)} %first_in.1) | copy-start | bytes 221188
  3.7 19.5 %copy-start.6 = (bf16[2,2,96,96]{3,2,1,0:T(8,128)(2,1)S(1)}, bf16[2,2,96,96]{3,2,1,0:T(8,128)(2,1)}, u32[]{:S(2)}) copy-start(bf16[2,2,96,96]{3,2,1,0:T(8,128)(2,1)} %second_in.1) | copy-start | bytes 221188
  3.7 19.5 %copy-start.7 = (bf16[2,2,96]{2,1,0:T(2,128)(2,1)S(1)}, bf16[2,2,96]{2,1,0:T(2,128)(2,1)}, u32[]{:S(2)}) copy-start(bf16[2,2,96]{2,1,0:T(2,128)(2,1)} %bias_in.1) | copy-start | bytes 2308
  3.7 12.8 %collective-permute-start = (bf16[64,768]{1,0:T(8,128)(2,1)S(1)}, bf16[64,768]{1,0:T(8,128)(2,1)S(1)}, u32[]{:S(2)}, u32[]{:S(2)}) collective-permute-start(bf16[64,768]{1,0:T(8,128)(2,1)S(1)} %get-tuple-element.31), channel_id=1, source_target_pairs={{0,28},{4,24},{8,20},{12,16},{16,12},{20,8},{24,4},{28,0},{1,29},{... | collective-permute-start | bytes 294920 | tf_op jit(solution)/shard_map/ppermute | solution.py:307
  11.7 15.1 %copy-start.3 = (bf16[256,256]{1,0:T(8,128)(2,1)S(1)}, bf16[256,256]{1,0:T(8,128)(2,1)}, u32[]{:S(2)}) copy-start(bf16[256,256]{1,0:T(8,128)(2,1)} %constant.11.clone.refs_9_) | copy-start | bytes 393220
  11.7 15.1 %copy-start.4 = (bf16[256,256]{1,0:T(8,128)(2,1)S(1)}, bf16[256,256]{1,0:T(8,128)(2,1)}, u32[]{:S(2)}) copy-start(bf16[256,256]{1,0:T(8,128)(2,1)} %constant.10.clone.refs_8_) | copy-start | bytes 393220
  11.8 10.5 %collective-permute-start.1 = (bf16[64,768]{1,0:T(8,128)(2,1)S(1)}, bf16[64,768]{1,0:T(8,128)(2,1)S(1)}, u32[]{:S(2)}, u32[]{:S(2)}) collective-permute-start(bf16[64,768]{1,0:T(8,128)(2,1)S(1)} %get-tuple-element.32), channel_id=1, source_target_pairs={{0,20},{4,16},{8,28},{12,24},{16,4},{20,0},{24,12},{28,8},{1,21},{... | collective-permute-start | bytes 294920 | tf_op jit(solution)/shard_map/ppermute | solution.py:307
  11.8 11.8 %collective-permute-start.2 = (bf16[64,768]{1,0:T(8,128)(2,1)S(1)}, bf16[64,768]{1,0:T(8,128)(2,1)S(1)}, u32[]{:S(2)}, u32[]{:S(2)}) collective-permute-start(bf16[64,768]{1,0:T(8,128)(2,1)S(1)} %get-tuple-element.33), channel_id=1, source_target_pairs={{0,24},{4,28},{8,16},{12,20},{16,8},{20,12},{24,0},{28,4},{1,25},{... | collective-permute-start | bytes 294920 | tf_op jit(solution)/shard_map/ppermute | solution.py:307
  13.7 10.0 %collective-permute-start.3 = (bf16[64,768]{1,0:T(8,128)(2,1)S(1)}, bf16[64,768]{1,0:T(8,128)(2,1)S(1)}, u32[]{:S(2)}, u32[]{:S(2)}) collective-permute-start(bf16[64,768]{1,0:T(8,128)(2,1)S(1)} %get-tuple-element.34), channel_id=1, source_target_pairs={{0,12},{4,8},{8,4},{12,0},{16,28},{20,24},{24,20},{28,16},{1,13},{... | collective-permute-start | bytes 294920 | tf_op jit(solution)/shard_map/ppermute | solution.py:307
  16.2 10.3 %collective-permute-start.4 = (bf16[64,768]{1,0:T(8,128)(2,1)S(1)}, bf16[64,768]{1,0:T(8,128)(2,1)S(1)}, u32[]{:S(2)}, u32[]{:S(2)}) collective-permute-start(bf16[64,768]{1,0:T(8,128)(2,1)S(1)} %get-tuple-element.35), channel_id=1, source_target_pairs={{0,16},{4,20},{8,24},{12,28},{16,0},{20,4},{24,8},{28,12},{1,17},{... | collective-permute-start | bytes 294920 | tf_op jit(solution)/shard_map/ppermute | solution.py:307
  16.6 10.0 %collective-permute-start.5 = (bf16[64,768]{1,0:T(8,128)(2,1)S(1)}, bf16[64,768]{1,0:T(8,128)(2,1)S(1)}, u32[]{:S(2)}, u32[]{:S(2)}) collective-permute-start(bf16[64,768]{1,0:T(8,128)(2,1)S(1)} %get-tuple-element.36), channel_id=1, source_target_pairs={{0,8},{4,12},{8,0},{12,4},{16,24},{20,28},{24,16},{28,20},{1,9},{5... | collective-permute-start | bytes 294920 | tf_op jit(solution)/shard_map/ppermute | solution.py:307
  22.2 4.6 %collective-permute-start.6 = (bf16[64,768]{1,0:T(8,128)(2,1)S(1)}, bf16[64,768]{1,0:T(8,128)(2,1)S(1)}, u32[]{:S(2)}, u32[]{:S(2)}) collective-permute-start(bf16[64,768]{1,0:T(8,128)(2,1)S(1)} %get-tuple-element.37), channel_id=1, source_target_pairs={{0,4},{4,0},{8,12},{12,8},{16,20},{20,16},{24,28},{28,24},{1,5},{5... | collective-permute-start | bytes 294920 | tf_op jit(solution)/shard_map/ppermute | solution.py:307
  26.9 22.6 %copy-start.2 = (bf16[768,512]{1,0:T(8,128)(2,1)S(1)}, bf16[768,512]{1,0:T(8,128)(2,1)}, u32[]{:S(2)}) copy-start(bf16[768,512]{1,0:T(8,128)(2,1)} %constant.8.clone.east_ref) | copy-start | bytes 2359300
  29.0 8.3 %collective-permute-start.7 = (bf16[272,128]{1,0:T(8,128)(2,1)S(1)}, bf16[272,128]{1,0:T(8,128)(2,1)S(1)}, u32[]{:S(2)}, u32[]{:S(2)}) collective-permute-start(bf16[272,128]{1,0:T(8,128)(2,1)S(1)} %get-tuple-element.43), channel_id=1, source_target_pairs={{0,20},{4,16},{8,28},{12,24},{16,4},{20,0},{24,12},{28,8},{1,21},{... | collective-permute-start | bytes 208904 | tf_op jit(solution)/shard_map/ppermute | solution.py:307
  29.2 8.3 %collective-permute-start.8 = (bf16[272,128]{1,0:T(8,128)(2,1)S(1)}, bf16[272,128]{1,0:T(8,128)(2,1)S(1)}, u32[]{:S(2)}, u32[]{:S(2)}) collective-permute-start(bf16[272,128]{1,0:T(8,128)(2,1)S(1)} %get-tuple-element.44), channel_id=1, source_target_pairs={{0,28},{4,24},{8,20},{12,16},{16,12},{20,8},{24,4},{28,0},{1,29},{... | collective-permute-start | bytes 208904 | tf_op jit(solution)/shard_map/ppermute | solution.py:307
  32.0 7.5 %collective-permute-start.9 = (bf16[272,128]{1,0:T(8,128)(2,1)S(1)}, bf16[272,128]{1,0:T(8,128)(2,1)S(1)}, u32[]{:S(2)}, u32[]{:S(2)}) collective-permute-start(bf16[272,128]{1,0:T(8,128)(2,1)S(1)} %get-tuple-element.45), channel_id=1, source_target_pairs={{0,12},{4,8},{8,4},{12,0},{16,28},{20,24},{24,20},{28,16},{1,13},{... | collective-permute-start | bytes 208904 | tf_op jit(solution)/shard_map/ppermute | solution.py:307
  34.1 9.0 %collective-permute-start.10 = (bf16[272,128]{1,0:T(8,128)(2,1)S(1)}, bf16[272,128]{1,0:T(8,128)(2,1)S(1)}, u32[]{:S(2)}, u32[]{:S(2)}) collective-permute-start(bf16[272,128]{1,0:T(8,128)(2,1)S(1)} %get-tuple-element.46), channel_id=1, source_target_pairs={{0,16},{4,20},{8,24},{12,28},{16,0},{20,4},{24,8},{28,12},{1,17},{... | collective-permute-start | bytes 208904 | tf_op jit(solution)/shard_map/ppermute | solution.py:307
  34.5 8.6 %collective-permute-start.11 = (bf16[272,128]{1,0:T(8,128)(2,1)S(1)}, bf16[272,128]{1,0:T(8,128)(2,1)S(1)}, u32[]{:S(2)}, u32[]{:S(2)}) collective-permute-start(bf16[272,128]{1,0:T(8,128)(2,1)S(1)} %get-tuple-element.47), channel_id=1, source_target_pairs={{0,24},{4,28},{8,16},{12,20},{16,8},{20,12},{24,0},{28,4},{1,25},{... | collective-permute-start | bytes 208904 | tf_op jit(solution)/shard_map/ppermute | solution.py:307
  37.3 5.9 %collective-permute-start.12 = (bf16[272,128]{1,0:T(8,128)(2,1)S(1)}, bf16[272,128]{1,0:T(8,128)(2,1)S(1)}, u32[]{:S(2)}, u32[]{:S(2)}) collective-permute-start(bf16[272,128]{1,0:T(8,128)(2,1)S(1)} %get-tuple-element.48), channel_id=1, source_target_pairs={{0,8},{4,12},{8,0},{12,4},{16,24},{20,28},{24,16},{28,20},{1,9},{5... | collective-permute-start | bytes 208904 | tf_op jit(solution)/shard_map/ppermute | solution.py:307
  37.5 5.7 %collective-permute-start.13 = (bf16[272,128]{1,0:T(8,128)(2,1)S(1)}, bf16[272,128]{1,0:T(8,128)(2,1)S(1)}, u32[]{:S(2)}, u32[]{:S(2)}) collective-permute-start(bf16[272,128]{1,0:T(8,128)(2,1)S(1)} %get-tuple-element.49), channel_id=1, source_target_pairs={{0,4},{4,0},{8,12},{12,8},{16,20},{20,16},{24,28},{28,24},{1,5},{5... | collective-permute-start | bytes 208904 | tf_op jit(solution)/shard_map/ppermute | solution.py:307
  44.0 13.0 %all-to-all-start = ((bf16[8,72,128]{2,1,0:T(8,128)(2,1)}), bf16[8,72,128]{2,1,0:T(8,128)(2,1)S(1)}, u32[]{:S(2)}, u32[]{:S(2)}) async-start(bf16[8,72,128]{2,1,0:T(8,128)(2,1)} %get-tuple-element.50), calls=%async_computation | async-start | bytes 294912 | tf_op jit(solution)/shard_map/all_to_all | solution.py:395
where the time goes:
time: 58 us; the launch traced here: 57.8 us
  starting transfers between devices  28.3 us (49%)
  waiting for transfers between devices  17.3 us (30%)
  Pallas kernels  11.3 us (19%)
  between operations  0.77 us (1%)
    ppermute x14, starting transfers between devices, swap(): got.append(lax.ppermute(piece, 'lat', pairs) if d else piece)  22.8 us
    ppermute x14, waiting for transfers between devices, swap(): got.append(lax.ppermute(piece, 'lat', pairs) if d else piece)  12.1 us
    pallas_call x7, Pallas kernels, call(): pl.pallas_call(kernel, out_shape=[jax.ShapeDtypeStruct(shape, kind) for s...  11.3 us
    all_to_all x1, starting transfers between devices, local(): lax.all_to_all(chunk, 'lat', split_axis=0, concat_axis=0, tiled=True)  5.5 us
    all_to_all x1, waiting for transfers between devices, local(): lax.all_to_all(chunk, 'lat', split_axis=0, concat_axis=0, tiled=True)  5.23 us
  transfers between devices with their start and end apart: 15, of which 7 were waited for; matrix products, arithmetic and copies ran while one was open for 0% of the time, Pallas kernels for 8%

commit v1 on v0

--- a/solution.py
+++ b/solution.py
@@ -6,13 +6,14 @@
 import numpy as np
 from jax import lax
 from jax.experimental import pallas as pl
+from jax.experimental.layout import Layout, with_layout_constraint
 from jax.experimental.pallas import tpu as pltpu
 from jax.sharding import PartitionSpec as P
 
 
 WAVES = 256
 PAIRWISE = (2, 4, 8)
-GO_ORDER = (0, 7, 5, 6, 3, 4, 2, 1)
+GO_ORDER = (0, 7, 5, 6, 3, 2, 4, 1)
 BACK_ORDER = (0, 5, 7, 3, 4, 6, 2, 1)
 BF16 = jnp.bfloat16
 F32 = jnp.float32
@@ -74,10 +75,10 @@
     products, biases = ([], []), []
     for n in range(blocks):
         modes, up = lay_ref[0, n], lay_ref[1, n] * shrink_ref[n]
-        keep = relu_ref[n].astype(F32)
+        keep = relu_ref[n]
         one, two = weight_ref[0, n], weight_ref[1, n]
-        hidden = (keep * (dot(modes, one) + bias_ref[n : n + 1, :].astype(F32))).astype(BF16)
-        inner = (keep * dot(up, two, COLS)).astype(BF16)
+        hidden = keep * (dot(modes, one) + bias_ref[n : n + 1, :].astype(F32)).astype(BF16)
+        inner = keep * dot(up, two, COLS).astype(BF16)
         lay_ref[0, n] = dot(inner, one, COLS).astype(BF16)
         products[0].append(dot(modes, inner, ROWS))
         products[1].append(dot(hidden, up, ROWS))
@@ -132,7 +133,7 @@
 def send_kernel(geo, tokens_ref, cotangent_ref, east_ref, out_ref, grid_ref,
                 flat_ref, fields_ref, table_ref, sems):
     owners, block, units, padded, tiles, unit = geo
-    rows, blocks = tokens_ref.shape[:2]
+    rows, blocks = tokens_ref.shape[0], tokens_ref.shape[1] // (units * tiles)
     field = rows * blocks * block
     span = out_ref.shape[0]
     copies = []
@@ -151,11 +152,13 @@
         places = []
         for h in range(rows):
             copies[f * rows + h].wait()
-            flat = fields_ref[f, h].astype(F32)
-            flat_ref[f, h] = flat.reshape(blocks, units * tiles, 128)
+            flat_ref[f, h] = fields_ref[f, h].astype(F32)
             for n in range(blocks):
-                parts = [flat_ref[f, h, n, pl.ds(c, units, stride=tiles), :].astype(BF16)
-                         for c in range(tiles)]
+                parts = [
+                    flat_ref[f, h, pl.ds(c * blocks + n, units, stride=tiles * blocks), :]
+                    for c in range(tiles)
+                ]
+                parts = [part.astype(BF16) for part in parts]
                 places.append(jnp.concatenate(parts, axis=1))
         for r in range(unit):
             piece = [place[:, r * block : (r + 1) * block] for place in places]
@@ -335,6 +338,11 @@
     forward = jnp.asarray(table, BF16)
     backward = jnp.asarray(table.T, BF16)
 
+    def by_tile(value):
+        value = value.reshape(rows, blocks, units * tiles, 128)
+        value = with_layout_constraint(value, Layout(major_to_minor=(0, 2, 1, 3)))
+        return value.transpose(0, 2, 1, 3).reshape(rows, blocks * units * tiles, 128)
+
     def by_mode(mask):
         mask = mask.astype(BF16).reshape(2, blocks, groups, group, north, block)
         return mask.transpose(1, 2, 4, 3, 0, 5).reshape(blocks, wave_dev * north, 2 * block)
@@ -356,9 +364,10 @@
     ahead = span if pairwise else owners * span
     waves, grid = call(
         functools.partial(send_kernel, geo),
-        [tokens.reshape(flat), cotangent.reshape(flat), east],
+        [by_tile(tokens), by_tile(cotangent), east],
         [(ahead, 2 * field), (unit * padded, 2 * field)],
-        [pltpu.VMEM((2, rows, blocks, units * tiles, 128), F32), pltpu.VMEM((2,) + flat, BF16),
+        [pltpu.VMEM((2, rows, blocks * units * tiles, 128), F32),
+         pltpu.VMEM((2, rows, blocks * units * tiles, 128), BF16),
          pltpu.VMEM((ahead, unit * padded), BF16), pltpu.SemaphoreType.DMA((2 * rows + 1,))],
         3,
     )

time: 58 us -> 57.2 us (0.986)
  waiting for transfers between devices: 17.3 us -> 15.7 us
  starting transfers between devices: 28.3 us -> 29.9 us
  Pallas kernels: 11.3 us -> 10.5 us
    ppermute x14, waiting for transfers between devices: 12.1 us -> 10.5 us  [swap(): got.append(lax.ppermute(piece, 'lat', pairs) if d else piece)]
    ppermute x14, starting transfers between devices: 22.8 us -> 24.2 us  [swap(): got.append(lax.ppermute(piece, 'lat', pairs) if d else piece)]
    pallas_call x7, Pallas kernels: 11.3 us -> 10.5 us  [call(): pl.pallas_call(kernel, out_shape=[jax.ShapeDtypeStruct(shape, kind) for s...]
where the time goes in v1:
time: 57.2 us; the launch traced here: 56.9 us
  starting transfers between devices  29.9 us (52%)
  waiting for transfers between devices  15.7 us (27%)
  Pallas kernels  10.5 us (18%)
  between operations  0.78 us (1%)
    ppermute x14, starting transfers between devices, swap(): got.append(lax.ppermute(piece, 'lat', pairs) if d else piece)  24.2 us
    ppermute x14, waiting for transfers between devices, swap(): got.append(lax.ppermute(piece, 'lat', pairs) if d else piece)  10.5 us
    pallas_call x7, Pallas kernels, call(): pl.pallas_call(kernel, out_shape=[jax.ShapeDtypeStruct(shape, kind) for s...  10.5 us
    all_to_all x1, starting transfers between devices, local(): lax.all_to_all(chunk, 'lat', split_axis=0, concat_axis=0, tiled=True)  5.7 us
    all_to_all x1, waiting for transfers between devices, local(): lax.all_to_all(chunk, 'lat', split_axis=0, concat_axis=0, tiled=True)  5.23 us
  transfers between devices with their start and end apart: 15, of which 7 were waited for; matrix products, arithmetic and copies ran while one was open for 0% of the time, Pallas kernels for 8%

profile of v1, /device:TPU:0, one launch (start us, length us, event | category | flops | bytes accessed | tf_op | source)
XLA Modules:
  0.0 56.9 jit_solution(2456564813091300083)
XLA Ops:
  0.6 2.1 %shard_map.138 = (bf16[64,768]{1,0:T(8,128)(2,1)S(1)}, bf16[768,768]{1,0:T(8,128)(2,1)S(1)}) custom-call(bf16[2,1080,128]{2,1,0:T(8,128)(2,1)} %bitcast.11, bf16[2,1080,128]{2,1,0:T(8,128)(2,1)} %bitcast.12, bf16[512,768]{1,0:T(8,128)(2,1)} %constant.9.clone.east_ref), custom_call_target="tpu_custom_call" | custom-call | tf_op jit(solution)/shard_map/pallas_call | solution.py:296
  2.8 6.1 %collective-permute-start = (bf16[64,768]{1,0:T(8,128)(2,1)S(1)}, bf16[64,768]{1,0:T(8,128)(2,1)S(1)}, u32[]{:S(2)}, u32[]{:S(2)}) collective-permute-start(bf16[64,768]{1,0:T(8,128)(2,1)S(1)} %get-tuple-element.31), channel_id=1, source_target_pairs={{0,28},{4,24},{8,20},{12,16},{16,12},{20,8},{24,4},{28,0},{1,29},{... | collective-permute-start | bytes 294920 | tf_op jit(solution)/shard_map/ppermute | solution.py:310
  8.9 1.9 %shard_map.139 = (bf16[64,768]{1,0:T(8,128)(2,1)S(1)}, bf16[64,768]{1,0:T(8,128)(2,1)S(1)}, bf16[64,768]{1,0:T(8,128)(2,1)S(1)}, bf16[64,768]{1,0:T(8,128)(2,1)S...) custom-call(bf16[512,768]{1,0:T(8,128)(2,1)} %constant.9.clone.east_ref, ...), custom_call_target="tpu_custom_call" | custom-call | tf_op jit(solution)/shard_map/pallas_call | solution.py:296
  11.0 1.9 %collective-permute-start.2 = (bf16[64,768]{1,0:T(8,128)(2,1)S(1)}, bf16[64,768]{1,0:T(8,128)(2,1)S(1)}, u32[]{:S(2)}, u32[]{:S(2)}) collective-permute-start(bf16[64,768]{1,0:T(8,128)(2,1)S(1)} %get-tuple-element.33), channel_id=1, source_target_pairs={{0,24},{4,28},{8,16},{12,20},{16,8},{20,12},{24,0},{28,4},{1,25},{... | collective-permute-start | bytes 294920 | tf_op jit(solution)/shard_map/ppermute | solution.py:310
  12.8 2.5 %collective-permute-start.3 = (bf16[64,768]{1,0:T(8,128)(2,1)S(1)}, bf16[64,768]{1,0:T(8,128)(2,1)S(1)}, u32[]{:S(2)}, u32[]{:S(2)}) collective-permute-start(bf16[64,768]{1,0:T(8,128)(2,1)S(1)} %get-tuple-element.34), channel_id=1, source_target_pairs={{0,12},{4,8},{8,4},{12,0},{16,28},{20,24},{24,20},{28,16},{1,13},{... | collective-permute-start | bytes 294920 | tf_op jit(solution)/shard_map/ppermute | solution.py:310
  15.8 2.1 %collective-permute-start.5 = (bf16[64,768]{1,0:T(8,128)(2,1)S(1)}, bf16[64,768]{1,0:T(8,128)(2,1)S(1)}, u32[]{:S(2)}, u32[]{:S(2)}) collective-permute-start(bf16[64,768]{1,0:T(8,128)(2,1)S(1)} %get-tuple-element.36), channel_id=1, source_target_pairs={{0,16},{4,20},{8,24},{12,28},{16,0},{20,4},{24,8},{28,12},{1,17},{... | collective-permute-start | bytes 294920 | tf_op jit(solution)/shard_map/ppermute | solution.py:310
  17.9 2.4 %collective-permute-done.1.refs_2_ = bf16[64,768]{1,0:T(8,128)(2,1)S(1)} collective-permute-done((bf16[64,768]{1,0:T(8,128)(2,1)S(1)}, bf16[64,768]{1,0:T(8,128)(2,1)S(1)}, u32[]{:S(2)}, u32[]{:S(2)}) %collective-permute-start.1) | collective-permute-done | bytes 98336 | tf_op jit(solution)/shard_map/ppermute | solution.py:310
  20.3 0.8 %collective-permute-start.6 = (bf16[64,768]{1,0:T(8,128)(2,1)S(1)}, bf16[64,768]{1,0:T(8,128)(2,1)S(1)}, u32[]{:S(2)}, u32[]{:S(2)}) collective-permute-start(bf16[64,768]{1,0:T(8,128)(2,1)S(1)} %get-tuple-element.37), channel_id=1, source_target_pairs={{0,4},{4,0},{8,12},{12,8},{16,20},{20,16},{24,28},{28,24},{1,5},{5... | collective-permute-start | bytes 294920 | tf_op jit(solution)/shard_map/ppermute | solution.py:310
  21.6 0.6 %collective-permute-done.3.refs_4_ = bf16[64,768]{1,0:T(8,128)(2,1)S(1)} collective-permute-done((bf16[64,768]{1,0:T(8,128)(2,1)S(1)}, bf16[64,768]{1,0:T(8,128)(2,1)S(1)}, u32[]{:S(2)}, u32[]{:S(2)}) %collective-permute-start.3) | collective-permute-done | bytes 98336 | tf_op jit(solution)/shard_map/ppermute | solution.py:310
  22.2 1.4 %collective-permute-done.4.refs_5_ = bf16[64,768]{1,0:T(8,128)(2,1)S(1)} collective-permute-done((bf16[64,768]{1,0:T(8,128)(2,1)S(1)}, bf16[64,768]{1,0:T(8,128)(2,1)S(1)}, u32[]{:S(2)}, u32[]{:S(2)}) %collective-permute-start.4) | collective-permute-done | bytes 98336 | tf_op jit(solution)/shard_map/ppermute | solution.py:310
  23.7 2.0 %collective-permute-done.5.refs_6_ = bf16[64,768]{1,0:T(8,128)(2,1)S(1)} collective-permute-done((bf16[64,768]{1,0:T(8,128)(2,1)S(1)}, bf16[64,768]{1,0:T(8,128)(2,1)S(1)}, u32[]{:S(2)}, u32[]{:S(2)}) %collective-permute-start.5) | collective-permute-done | bytes 98336 | tf_op jit(solution)/shard_map/ppermute | solution.py:310
  25.7 2.2 %shard_map.141 = (bf16[272,128]{1,0:T(8,128)(2,1)S(1)}, bf16[272,128]{1,0:T(8,128)(2,1)S(1)}, bf16[272,128]{1,0:T(8,128)(2,1)S(1)}, bf16[272,128]{1,0:T(8,128)(2...) custom-call(bf16[64,768]{1,0:T(8,128)(2,1)S(1)} %get-tuple-element.3, ...), custom_call_target="tpu_custom_call" | custom-call | tf_op jit(solution)/shard_map/pallas_call | solution.py:296
  27.9 0.5 collective-permute-start.7
  28.4 2.5 %collective-permute-start.8 = (bf16[272,128]{1,0:T(8,128)(2,1)S(1)}, bf16[272,128]{1,0:T(8,128)(2,1)S(1)}, u32[]{:S(2)}, u32[]{:S(2)}) collective-permute-start(bf16[272,128]{1,0:T(8,128)(2,1)S(1)} %get-tuple-element.44), channel_id=1, source_target_pairs={{0,28},{4,24},{8,20},{12,16},{16,12},{20,8},{24,4},{28,0},{1,29},{... | collective-permute-start | bytes 208904 | tf_op jit(solution)/shard_map/ppermute | solution.py:310
  30.9 2.3 %collective-permute-start.9 = (bf16[272,128]{1,0:T(8,128)(2,1)S(1)}, bf16[272,128]{1,0:T(8,128)(2,1)S(1)}, u32[]{:S(2)}, u32[]{:S(2)}) collective-permute-start(bf16[272,128]{1,0:T(8,128)(2,1)S(1)} %get-tuple-element.45), channel_id=1, source_target_pairs={{0,12},{4,8},{8,4},{12,0},{16,28},{20,24},{24,20},{28,16},{1,13},{... | collective-permute-start | bytes 208904 | tf_op jit(solution)/shard_map/ppermute | solution.py:310
  33.6 2.2 %collective-permute-start.11 = (bf16[272,128]{1,0:T(8,128)(2,1)S(1)}, bf16[272,128]{1,0:T(8,128)(2,1)S(1)}, u32[]{:S(2)}, u32[]{:S(2)}) collective-permute-start(bf16[272,128]{1,0:T(8,128)(2,1)S(1)} %get-tuple-element.47), channel_id=1, source_target_pairs={{0,24},{4,28},{8,16},{12,20},{16,8},{20,12},{24,0},{28,4},{1,25},{... | collective-permute-start | bytes 208904 | tf_op jit(solution)/shard_map/ppermute | solution.py:310
  35.8 0.5 collective-permute-done.7.refs_1_
  36.7 1.9 %collective-permute-start.13 = (bf16[272,128]{1,0:T(8,128)(2,1)S(1)}, bf16[272,128]{1,0:T(8,128)(2,1)S(1)}, u32[]{:S(2)}, u32[]{:S(2)}) collective-permute-start(bf16[272,128]{1,0:T(8,128)(2,1)S(1)} %get-tuple-element.49), channel_id=1, source_target_pairs={{0,4},{4,0},{8,12},{12,8},{16,20},{20,16},{24,28},{28,24},{1,5},{5... | collective-permute-start | bytes 208904 | tf_op jit(solution)/shard_map/ppermute | solution.py:310
  38.6 3.6 %collective-permute-done.10.refs_4_ = bf16[272,128]{1,0:T(8,128)(2,1)S(1)} collective-permute-done((bf16[272,128]{1,0:T(8,128)(2,1)S(1)}, bf16[272,128]{1,0:T(8,128)(2,1)S(1)}, u32[]{:S(2)}, u32[]{:S(2)}) %collective-permute-start.10) | collective-permute-done | bytes 69664 | tf_op jit(solution)/shard_map/ppermute | solution.py:310
  42.2 0.7 %shard_map.143 = (bf16[8,72,128]{2,1,0:T(8,128)(2,1)}, f32[2,2,96]{2,1,0:T(2,128)}) custom-call(bf16[272,128]{1,0:T(8,128)(2,1)S(1)} %get-tuple-element.42.refs_0_, bf16[272,128]{1,0:T(8,128)(2,1)S(1)} %collective-permute-done.7.refs_1_, bf16[272,128]{1,0:T(8,128)(2,1)S(1)} %collective-permute-done.8.refs_2_, ...), custom_call_target="tpu_custom_call" | custom-call | tf_op jit(solution)/shard_map/pallas_call | solution.py:296
  42.9 5.7 %all-to-all-start = ((bf16[8,72,128]{2,1,0:T(8,128)(2,1)}), bf16[8,72,128]{2,1,0:T(8,128)(2,1)S(1)}, u32[]{:S(2)}, u32[]{:S(2)}) async-start(bf16[8,72,128]{2,1,0:T(8,128)(2,1)} %get-tuple-element.50), calls=%async_computation | async-start | bytes 294912 | tf_op jit(solution)/shard_map/all_to_all | solution.py:404
  48.7 2.2 %shard_map.142 = bf16[2,2,69120]{2,1,0:T(2,128)(2,1)} custom-call(bf16[768,512]{1,0:T(8,128)(2,1)S(1)} %copy-done.2, bf16[768,768]{1,0:T(8,128)(2,1)S(1)} %get-tuple-element.29.grid_ref, bf16[272,128]{1,0:T(8,128)(2,1)S(1)} %get-tuple-element.42.refs_0_, bf16[272,128]{1,0:T(8,128)(2,1)S(1)} %collective-permute-done.7.refs_1_, ...), custom_call_target="tpu_custom_call" | custom-call | tf_op jit(solution)/shard_map/pallas_call | solution.py:296
  50.9 5.2 %all-to-all-done.total_ref = bf16[8,72,128]{2,1,0:T(8,128)(2,1)S(1)} async-done(((bf16[8,72,128]{2,1,0:T(8,128)(2,1)}), bf16[8,72,128]{2,1,0:T(8,128)(2,1)S(1)}, u32[]{:S(2)}, u32[]{:S(2)}) %all-to-all-start) | async-done | bytes 147488 | tf_op jit(solution)/shard_map/all_to_all | solution.py:404
  56.1 0.8 %shard_map.144 = (f32[2,2,96,96]{3,2,1,0:T(8,128)}, f32[2,2,96,96]{3,2,1,0:T(8,128)}) custom-call(bf16[8,72,128]{2,1,0:T(8,128)(2,1)S(1)} %all-to-all-done.total_ref), custom_call_target="tpu_custom_call" | custom-call | tf_op jit(solution)/shard_map/pallas_call | solution.py:296
  (29 shorter events, 1.9 us)
Async XLA Ops:
  2.8 18.4 %copy-start = (s32[1,2,2,32,1536]{4,3,2,1,0:T(8,128)S(1)}, s32[1,2,2,32,1536]{4,3,2,1,0:T(8,128)}, u32[]{:S(2)}) copy-start(s32[1,2,2,32,1536]{4,3,2,1,0:T(8,128)} %relu_in.1) | copy-start | bytes 2359300
  2.8 18.4 %copy-start.1 = (s32[1,2,2,32,1536]{4,3,2,1,0:T(8,128)S(1)}, s32[1,2,2,32,1536]{4,3,2,1,0:T(8,128)}, u32[]{:S(2)}) copy-start(s32[1,2,2,32,1536]{4,3,2,1,0:T(8,128)} %shrink_in.1) | copy-start | bytes 2359300
  2.8 18.4 %copy-start.5 = (bf16[2,2,96,96]{3,2,1,0:T(8,128)(2,1)S(1)}, bf16[2,2,96,96]{3,2,1,0:T(8,128)(2,1)}, u32[]{:S(2)}) copy-start(bf16[2,2,96,96]{3,2,1,0:T(8,128)(2,1)} %first_in.1) | copy-start | bytes 221188
  2.8 18.3 %copy-start.6 = (bf16[2,2,96,96]{3,2,1,0:T(8,128)(2,1)S(1)}, bf16[2,2,96,96]{3,2,1,0:T(8,128)(2,1)}, u32[]{:S(2)}) copy-start(bf16[2,2,96,96]{3,2,1,0:T(8,128)(2,1)} %second_in.1) | copy-start | bytes 221188
  2.8 18.3 %copy-start.7 = (bf16[2,2,96]{2,1,0:T(2,128)(2,1)S(1)}, bf16[2,2,96]{2,1,0:T(2,128)(2,1)}, u32[]{:S(2)}) copy-start(bf16[2,2,96]{2,1,0:T(2,128)(2,1)} %bias_in.1) | copy-start | bytes 2308
  2.8 13.0 %collective-permute-start = (bf16[64,768]{1,0:T(8,128)(2,1)S(1)}, bf16[64,768]{1,0:T(8,128)(2,1)S(1)}, u32[]{:S(2)}, u32[]{:S(2)}) collective-permute-start(bf16[64,768]{1,0:T(8,128)(2,1)S(1)} %get-tuple-element.31), channel_id=1, source_target_pairs={{0,28},{4,24},{8,20},{12,16},{16,12},{20,8},{24,4},{28,0},{1,29},{... | collective-permute-start | bytes 294920 | tf_op jit(solution)/shard_map/ppermute | solution.py:310
  10.9 14.8 %copy-start.3 = (bf16[256,256]{1,0:T(8,128)(2,1)S(1)}, bf16[256,256]{1,0:T(8,128)(2,1)}, u32[]{:S(2)}) copy-start(bf16[256,256]{1,0:T(8,128)(2,1)} %constant.11.clone.refs_9_) | copy-start | bytes 393220
  10.9 14.8 %copy-start.4 = (bf16[256,256]{1,0:T(8,128)(2,1)S(1)}, bf16[256,256]{1,0:T(8,128)(2,1)}, u32[]{:S(2)}) copy-start(bf16[256,256]{1,0:T(8,128)(2,1)} %constant.10.clone.refs_8_) | copy-start | bytes 393220
  10.9 9.4 %collective-permute-start.1 = (bf16[64,768]{1,0:T(8,128)(2,1)S(1)}, bf16[64,768]{1,0:T(8,128)(2,1)S(1)}, u32[]{:S(2)}, u32[]{:S(2)}) collective-permute-start(bf16[64,768]{1,0:T(8,128)(2,1)S(1)} %get-tuple-element.32), channel_id=1, source_target_pairs={{0,20},{4,16},{8,28},{12,24},{16,4},{20,0},{24,12},{28,8},{1,21},{... | collective-permute-start | bytes 294920 | tf_op jit(solution)/shard_map/ppermute | solution.py:310
  11.0 10.6 %collective-permute-start.2 = (bf16[64,768]{1,0:T(8,128)(2,1)S(1)}, bf16[64,768]{1,0:T(8,128)(2,1)S(1)}, u32[]{:S(2)}, u32[]{:S(2)}) collective-permute-start(bf16[64,768]{1,0:T(8,128)(2,1)S(1)} %get-tuple-element.33), channel_id=1, source_target_pairs={{0,24},{4,28},{8,16},{12,20},{16,8},{20,12},{24,0},{28,4},{1,25},{... | collective-permute-start | bytes 294920 | tf_op jit(solution)/shard_map/ppermute | solution.py:310
  12.8 9.4 %collective-permute-start.3 = (bf16[64,768]{1,0:T(8,128)(2,1)S(1)}, bf16[64,768]{1,0:T(8,128)(2,1)S(1)}, u32[]{:S(2)}, u32[]{:S(2)}) collective-permute-start(bf16[64,768]{1,0:T(8,128)(2,1)S(1)} %get-tuple-element.34), channel_id=1, source_target_pairs={{0,12},{4,8},{8,4},{12,0},{16,28},{20,24},{24,20},{28,16},{1,13},{... | collective-permute-start | bytes 294920 | tf_op jit(solution)/shard_map/ppermute | solution.py:310
  15.3 8.3 %collective-permute-start.4 = (bf16[64,768]{1,0:T(8,128)(2,1)S(1)}, bf16[64,768]{1,0:T(8,128)(2,1)S(1)}, u32[]{:S(2)}, u32[]{:S(2)}) collective-permute-start(bf16[64,768]{1,0:T(8,128)(2,1)S(1)} %get-tuple-element.35), channel_id=1, source_target_pairs={{0,8},{4,12},{8,0},{12,4},{16,24},{20,28},{24,16},{28,20},{1,9},{5... | collective-permute-start | bytes 294920 | tf_op jit(solution)/shard_map/ppermute | solution.py:310
  15.8 9.9 %collective-permute-start.5 = (bf16[64,768]{1,0:T(8,128)(2,1)S(1)}, bf16[64,768]{1,0:T(8,128)(2,1)S(1)}, u32[]{:S(2)}, u32[]{:S(2)}) collective-permute-start(bf16[64,768]{1,0:T(8,128)(2,1)S(1)} %get-tuple-element.36), channel_id=1, source_target_pairs={{0,16},{4,20},{8,24},{12,28},{16,0},{20,4},{24,8},{28,12},{1,17},{... | collective-permute-start | bytes 294920 | tf_op jit(solution)/shard_map/ppermute | solution.py:310
  20.3 5.4 %collective-permute-start.6 = (bf16[64,768]{1,0:T(8,128)(2,1)S(1)}, bf16[64,768]{1,0:T(8,128)(2,1)S(1)}, u32[]{:S(2)}, u32[]{:S(2)}) collective-permute-start(bf16[64,768]{1,0:T(8,128)(2,1)S(1)} %get-tuple-element.37), channel_id=1, source_target_pairs={{0,4},{4,0},{8,12},{12,8},{16,20},{20,16},{24,28},{28,24},{1,5},{5... | collective-permute-start | bytes 294920 | tf_op jit(solution)/shard_map/ppermute | solution.py:310
  25.7 23.0 %copy-start.2 = (bf16[768,512]{1,0:T(8,128)(2,1)S(1)}, bf16[768,512]{1,0:T(8,128)(2,1)}, u32[]{:S(2)}) copy-start(bf16[768,512]{1,0:T(8,128)(2,1)} %constant.8.clone.east_ref) | copy-start | bytes 2359300
  27.9 8.4 %collective-permute-start.7 = (bf16[272,128]{1,0:T(8,128)(2,1)S(1)}, bf16[272,128]{1,0:T(8,128)(2,1)S(1)}, u32[]{:S(2)}, u32[]{:S(2)}) collective-permute-start(bf16[272,128]{1,0:T(8,128)(2,1)S(1)} %get-tuple-element.43), channel_id=1, source_target_pairs={{0,20},{4,16},{8,28},{12,24},{16,4},{20,0},{24,12},{28,8},{1,21},{... | collective-permute-start | bytes 208904 | tf_op jit(solution)/shard_map/ppermute | solution.py:310
  28.4 8.3 %collective-permute-start.8 = (bf16[272,128]{1,0:T(8,128)(2,1)S(1)}, bf16[272,128]{1,0:T(8,128)(2,1)S(1)}, u32[]{:S(2)}, u32[]{:S(2)}) collective-permute-start(bf16[272,128]{1,0:T(8,128)(2,1)S(1)} %get-tuple-element.44), channel_id=1, source_target_pairs={{0,28},{4,24},{8,20},{12,16},{16,12},{20,8},{24,4},{28,0},{1,29},{... | collective-permute-start | bytes 208904 | tf_op jit(solution)/shard_map/ppermute | solution.py:310
  30.9 7.7 %collective-permute-start.9 = (bf16[272,128]{1,0:T(8,128)(2,1)S(1)}, bf16[272,128]{1,0:T(8,128)(2,1)S(1)}, u32[]{:S(2)}, u32[]{:S(2)}) collective-permute-start(bf16[272,128]{1,0:T(8,128)(2,1)S(1)} %get-tuple-element.45), channel_id=1, source_target_pairs={{0,12},{4,8},{8,4},{12,0},{16,28},{20,24},{24,20},{28,16},{1,13},{... | collective-permute-start | bytes 208904 | tf_op jit(solution)/shard_map/ppermute | solution.py:310
  33.2 9.0 %collective-permute-start.10 = (bf16[272,128]{1,0:T(8,128)(2,1)S(1)}, bf16[272,128]{1,0:T(8,128)(2,1)S(1)}, u32[]{:S(2)}, u32[]{:S(2)}) collective-permute-start(bf16[272,128]{1,0:T(8,128)(2,1)S(1)} %get-tuple-element.46), channel_id=1, source_target_pairs={{0,16},{4,20},{8,24},{12,28},{16,0},{20,4},{24,8},{28,12},{1,17},{... | collective-permute-start | bytes 208904 | tf_op jit(solution)/shard_map/ppermute | solution.py:310
  33.6 8.6 %collective-permute-start.11 = (bf16[272,128]{1,0:T(8,128)(2,1)S(1)}, bf16[272,128]{1,0:T(8,128)(2,1)S(1)}, u32[]{:S(2)}, u32[]{:S(2)}) collective-permute-start(bf16[272,128]{1,0:T(8,128)(2,1)S(1)} %get-tuple-element.47), channel_id=1, source_target_pairs={{0,24},{4,28},{8,16},{12,20},{16,8},{20,12},{24,0},{28,4},{1,25},{... | collective-permute-start | bytes 208904 | tf_op jit(solution)/shard_map/ppermute | solution.py:310
  36.3 5.9 %collective-permute-start.12 = (bf16[272,128]{1,0:T(8,128)(2,1)S(1)}, bf16[272,128]{1,0:T(8,128)(2,1)S(1)}, u32[]{:S(2)}, u32[]{:S(2)}) collective-permute-start(bf16[272,128]{1,0:T(8,128)(2,1)S(1)} %get-tuple-element.48), channel_id=1, source_target_pairs={{0,8},{4,12},{8,0},{12,4},{16,24},{20,28},{24,16},{28,20},{1,9},{5... | collective-permute-start | bytes 208904 | tf_op jit(solution)/shard_map/ppermute | solution.py:310
  36.7 5.5 %collective-permute-start.13 = (bf16[272,128]{1,0:T(8,128)(2,1)S(1)}, bf16[272,128]{1,0:T(8,128)(2,1)S(1)}, u32[]{:S(2)}, u32[]{:S(2)}) collective-permute-start(bf16[272,128]{1,0:T(8,128)(2,1)S(1)} %get-tuple-element.49), channel_id=1, source_target_pairs={{0,4},{4,0},{8,12},{12,8},{16,20},{20,16},{24,28},{28,24},{1,5},{5... | collective-permute-start | bytes 208904 | tf_op jit(solution)/shard_map/ppermute | solution.py:310
  42.9 13.2 %all-to-all-start = ((bf16[8,72,128]{2,1,0:T(8,128)(2,1)}), bf16[8,72,128]{2,1,0:T(8,128)(2,1)S(1)}, u32[]{:S(2)}, u32[]{:S(2)}) async-start(bf16[8,72,128]{2,1,0:T(8,128)(2,1)} %get-tuple-element.50), calls=%async_computation | async-start | bytes 294912 | tf_op jit(solution)/shard_map/all_to_all | solution.py:404
